TPU v7x, 256 devices: a whole 4x4x8 slice. The times are simulated.
256 devices in a mesh: sub: 64 (over x, z, core), crs: 4 (over y).
Axes of the slice: x: 4, y: 4, z: 8, core: 2. Of those that a mesh axis runs over, the one named last changes fastest.
Arguments:
- residual: float32 [256, 6, 3072], P('sub', None, 'crs'), may hold values from -6 to 6
- stiffness: float32 [256, 6, 3072], P('sub', None, 'crs'), may hold values from 0.1 to 10
- solid: int32 [256, 6, 16], P('sub', None, 'crs'), may hold values 0 or 1
- inverses: bfloat16 [256, 6, 192, 3072], P('sub', None, None, 'crs')
- coarse_basis: bfloat16 [256, 24, 6, 3072], P('sub', None, None, 'crs'), may hold values from -0.29882812 to 0.29882812
- assign: int32 [256], replicated, may hold values from 0 to 255, as said below
- corners: int32 [256, 8], P('sub'), may hold values from 0 to 255, as said below
- coarse_inverse: float32 [768, 768], P('crs')
Outputs:
- preconditioned: float32 [256, 6, 3072], P('sub', None, 'crs')
- inner_value: float32 [1], replicated
Inputs may be any that keep to these rules, and one draw needn't show every extreme that they name: assign is a permutation of the 256 subdomain numbers, set at run time by the load balancer, so a subdomain's neighbours may be held on any devices. corners[t, c] is the number of corner c = 4 cx + 2 cy + cz of subdomain assign[t], the grid vertex at its place plus (cx, cy, cz) taken periodically, under one fixed permutation of the 256 vertices.
All inputs are finite; a program needn't handle non-finite values. No bound on the sum of `solid` on one device may be relied on, other than what follows from the above.
Results may differ from a plain program's by a relative error of at most 0.0028.
Values sent between devices are 32-bit elements; how exact they have to be, the bound alone decides.
No kernel may reach another device: no remote copies, remote signals or barrier semaphores. Data moves between devices by JAX's collectives and lax.ppermute only.
A program may use at most 128 MiB of HBM per device.

v0:
```python
import jax
import jax.numpy as jnp
from jax import lax
from jax.sharding import PartitionSpec as P


def partner_rows(assign, subs):
    depth = subs // 16
    slots = jnp.arange(subs, dtype=jnp.int32)
    inverse = jnp.sum(
        slots[:, None] * (assign[:, None] == slots[None, :]).astype(jnp.int32), axis=0
    )
    coord_a = assign // (4 * depth)
    coord_b = assign // depth % 4
    coord_c = assign % depth

    def number(first, second, third):
        return (first * 4 + second) * depth + third

    neighbours = jnp.stack(
        [
            number((coord_a + 1) % 4, coord_b, coord_c),
            number(coord_a, (coord_b + 1) % 4, coord_c),
            number(coord_a, coord_b, (coord_c + 1) % depth),
            number((coord_a + 3) % 4, coord_b, coord_c),
            number(coord_a, (coord_b + 3) % 4, coord_c),
            number(coord_a, coord_b, (coord_c + depth - 1) % depth),
        ],
        axis=1,
    )
    partner_slot = jnp.sum(
        inverse[None, None, :] * (neighbours[:, :, None] == slots[None, None, :]).astype(jnp.int32),
        axis=2,
    )
    partner_face = jnp.array([3, 4, 5, 0, 1, 2], dtype=jnp.int32)
    return (partner_slot * 6 + partner_face[None, :]).reshape(-1)


def body(residual, stiffness, solid, inverses, coarse_basis, assign, corners, coarse_inverse):
    slots_here, faces, width_here = residual.shape
    patches_here = solid.shape[2]
    entries = width_here // patches_here
    columns = lax.axis_size("crs")
    subs = assign.shape[0]
    face_rows = slots_here * faces
    rows = partner_rows(assign, subs)
    position = lax.axis_index("sub")
    own_rows = lax.dynamic_slice_in_dim(rows, position * face_rows, face_rows)
    flat_r = residual.reshape(face_rows, -1)
    flat_k = stiffness.reshape(face_rows, -1)
    solid_f = jnp.repeat(solid.astype(jnp.float32), entries, axis=2)
    all_r, all_k = (
        lax.all_gather(flat_r, "sub", axis=0, tiled=True),
        lax.all_gather(flat_k, "sub", axis=0, tiled=True),
    )
    partner_k = all_k[own_rows]
    weight = flat_k / (flat_k + partner_k)
    weight_partner = partner_k / (flat_k + partner_k)
    restricted_flat = weight * (flat_r + all_r[own_rows])
    restricted = (solid_f * restricted_flat.reshape(residual.shape)).astype(jnp.bfloat16)
    blocks = inverses.reshape(slots_here, faces, entries, patches_here, entries)
    vectors = restricted.reshape(slots_here, faces, patches_here, entries)
    local = jnp.einsum(
        "sfipj,sfpj->sfpi", blocks, vectors, preferred_element_type=jnp.float32
    ).reshape(residual.shape)
    coarse_part = jnp.einsum(
        "scfk,sfk->sc", coarse_basis, restricted, preferred_element_type=jnp.float32
    )
    total_coarse = 3 * subs
    index = (3 * corners[:, :, None] + jnp.arange(3, dtype=jnp.int32)[None, None, :]).reshape(
        slots_here, 24
    )
    onehot = (index[:, :, None] == jnp.arange(total_coarse, dtype=jnp.int32)[None, None, :]).astype(
        jnp.float32
    )
    coarse_local = jnp.einsum("sc,scn->n", coarse_part, onehot, precision=lax.Precision.HIGHEST)
    coarse_residual = lax.psum(coarse_local, ("sub", "crs"))
    block_width = total_coarse // columns
    start = lax.axis_index("crs") * block_width
    block_part = lax.dynamic_slice_in_dim(coarse_residual, start, block_width)
    terms = jnp.dot(block_part, coarse_inverse, precision=lax.Precision.HIGHEST)
    coarse_solution = lax.psum(terms, "crs")
    corner_values = jnp.einsum(
        "scn,n->sc", onehot, coarse_solution, precision=lax.Precision.HIGHEST
    ).astype(jnp.bfloat16)
    correction = jnp.einsum(
        "sc,scfk->sfk", corner_values, coarse_basis, preferred_element_type=jnp.float32
    )
    solution = solid_f * (local + correction)
    flat_u = solution.reshape(face_rows, -1)
    all_u = lax.all_gather(flat_u, "sub", axis=0, tiled=True)
    averaged = weight * flat_u + weight_partner * all_u[own_rows]
    preconditioned = averaged.reshape(residual.shape)
    inner_value = lax.psum(jnp.sum(residual * preconditioned), ("sub", "crs")).reshape(1)
    return (preconditioned, inner_value)


def solution(mesh):
    return jax.shard_map(
        body,
        mesh=mesh,
        in_specs=(
            P("sub", None, "crs"),
            P("sub", None, "crs"),
            P("sub", None, "crs"),
            P("sub", None, None, "crs"),
            P("sub", None, None, "crs"),
            P(),
            P("sub", None),
            P("crs", None),
        ),
        out_specs=(P("sub", None, "crs"), P()),
        check_vma=False,
    )
```

profile of v0, /device:TPU:1, one launch (start us, length us, event | category | flops | bytes accessed | tf_op | source)
XLA Modules:
  0.0 431.3 jit_solution(17880507166367437837)
XLA Ops:
  7.2 0.0 copy-start
  7.2 0.0 all-gather.4.cloned.1.call-start
  7.2 1.0 copy.44
  8.2 0.6 reshape.60
  8.8 0.0 all-gather.4.cloned.1.call-update
  8.9 0.0 all-gather.6.cloned.1.call-start
  8.9 0.9 copy.47
  9.8 0.6 reshape.62
  10.5 0.0 all-gather.6.cloned.1.call-update
  10.5 0.0 all-gather.8.cloned.1.call-start
  10.5 0.7 fusion.12
  11.3 0.8 select_reduce_fusion.1
  12.1 0.5 select_reduce_fusion
  12.6 0.7 multiply_add_fusion
  13.3 0.1 copy.42
  13.5 0.1 add.184
  13.6 0.7 convert_element_type.12
  14.3 0.1 copy.45
  14.4 0.1 broadcast_in_dim.5
  14.5 0.1 reshape.61
  14.7 11.4 %copy.63 = bf16[4,6,192,768]{2,3,1,0:T(8,128)(2,1)} copy(bf16[4,6,192,768]{3,2,1,0:T(8,128)(2,1)} %param.12) | data formatting | bytes 14155776 | tf_op jit(solution)/shard_map/reshape | solution.py:61
  26.1 0.1 add.189
  26.2 0.1 add.190
  26.3 0.1 add.192
  26.4 0.1 compare_select_fusion
  26.4 68.0 %all-gather.4.cloned.1.call-done = f32[1536,768]{1,0:T(8,128)} async-done(((f32[24,768]{1,0:T(8,128)}), f32[1536,768]{1,0:T(8,128)}) %all-gather.4.cloned.1.call-update) | async-done | bytes 4718608 | tf_op jit(solution)/shard_map/all_gather | solution.py:54
  94.5 3.0 gather_fusion
  97.5 77.1 %all-gather.6.cloned.1.call-done = f32[1536,768]{1,0:T(8,128)} async-done(((f32[24,768]{1,0:T(8,128)}), f32[1536,768]{1,0:T(8,128)}) %all-gather.6.cloned.1.call-update) | async-done | bytes 4718608 | tf_op jit(solution)/shard_map/all_gather | solution.py:53
  174.5 3.0 gather_fusion.1
  177.5 0.1 fusion.3
  177.6 0.1 reshape.108
  177.7 5.1 %fusion.25 = f32[4,6,4,1,192]{4,3,2,1,0:T(1,128)S(1)} fusion(bf16[4,6,4,192,1]{3,4,2,1,0:T(2,128)(2,1)S(1)} %reshape.108, bf16[4,6,192,4,192]{2,4,3,1,0:T(8,128)(2,1)} %bitcast.41), kind=kOutput, calls=%fused_computation.85 | convolution fusion | flops 7077888 | bytes 7188480 | tf_op jit(solution)/shard_map/sfipj,sfpj->sfpi/dot_general | solution.py:63
  182.9 0.1 reshape.65
  183.0 0.4 convolution_bitcast_fusion
  183.4 0.3 convolution_reduce_fusion.1
  183.7 75.2 %psum.21 = f32[768]{0:T(1024)S(1)} all-reduce(f32[768]{0:T(1024)S(1)} %convolution_reduce_fusion.1), channel_id=1, replica_groups=mesh['sub'=64,'crs'=4] {'sub','crs'}, use_global_device_ids=true, to_apply=%region_2.3 | all-reduce | flops 768 | bytes 6144 | tf_op jit(solution)/shard_map/psum | solution.py:77
  258.9 0.1 dynamic_slice.7
  259.0 0.4 convolution_reduce_fusion
  259.4 7.2 %psum.22 = f32[768]{0:T(1024)S(1)} all-reduce(f32[768]{0:T(1024)S(1)} %convolution_reduce_fusion), channel_id=1, replica_groups=mesh['sub'=64,'crs'=4] {'crs'}, use_global_device_ids=true, to_apply=%region_3.4 | all-reduce | flops 768 | bytes 6144 | tf_op jit(solution)/shard_map/psum | solution.py:82
  266.6 0.5 fusion
  267.2 0.3 fusion.7
  267.5 0.6 reshape.66
  268.1 0.0 all-gather.8.cloned.1.call-update
  268.2 77.2 %all-gather.8.cloned.1.call-done = f32[1536,768]{1,0:T(8,128)} async-done(((f32[24,768]{1,0:T(8,128)}), f32[1536,768]{1,0:T(8,128)}) %all-gather.8.cloned.1.call-update) | async-done | bytes 4718608 | tf_op jit(solution)/shard_map/all_gather | solution.py:91
  345.4 3.0 gather_fusion.2
  348.3 0.7 multiply_reduce_fusion
  349.0 0.7 copy.53
  349.7 75.1 %psum.23 = f32[1]{0:T(128)} all-reduce(f32[1]{0:T(128)} %bitcast.18), channel_id=1, replica_groups=mesh['sub'=64,'crs'=4] {'sub','crs'}, use_global_device_ids=true, to_apply=%region_5.6 | all-reduce | flops 1 | bytes 8 | tf_op jit(solution)/shard_map/psum | solution.py:94
  (22 shorter events, 0.2 us)
Async XLA Ops:
  7.2 175.8 %copy-start = (bf16[4,24,6,768]{3,1,2,0:T(8,128)(2,1)S(1)}, bf16[4,24,6,768]{3,1,2,0:T(8,128)(2,1)}, u32[]{:S(2)}) copy-start(bf16[4,24,6,768]{3,1,2,0:T(8,128)(2,1)} %param.13) | copy-start | bytes 2654212
  7.2 87.3 %all-gather.4.cloned.1.call-start = ((), (), s32[]{:S(2)}) async-start(), calls=%async_computation | async-start | bytes 4792320 | tf_op jit(solution)/shard_map/all_gather | solution.py:54
  8.9 165.7 %all-gather.6.cloned.1.call-start = ((), (), s32[]{:S(2)}) async-start(), calls=%async_computation.1 | async-start | bytes 4792320 | tf_op jit(solution)/shard_map/all_gather | solution.py:53
  10.5 334.9 %all-gather.8.cloned.1.call-start = ((), (), s32[]{:S(2)}) async-start(), calls=%async_computation.2 | async-start | bytes 4792320 | tf_op jit(solution)/shard_map/all_gather | solution.py:91
  14.7 11.4 %copy-start.4 = (s32[4,8]{1,0:T(4,128)S(1)}, s32[4,8]{1,0:T(4,128)}, u32[]{:S(2)}) copy-start(s32[4,8]{1,0:T(4,128)} %param.15) | copy-start | bytes 388
  14.7 162.9 %copy-start.1 = (f32[4,6,768]{2,0,1:T(4,128)S(1)}, f32[4,6,768]{2,0,1:T(4,128)}, u32[]{:S(2)}) copy-start(f32[4,6,768]{2,0,1:T(4,128)} %param.9) | copy-start | bytes 221188
  14.7 162.9 %copy-start.2 = (f32[4,6,768]{2,0,1:T(4,128)S(1)}, f32[4,6,768]{2,0,1:T(4,128)}, u32[]{:S(2)}) copy-start(f32[4,6,768]{2,0,1:T(4,128)} %param.10) | copy-start | bytes 221188
  177.7 81.3 %copy-start.3 = (f32[192,768]{1,0:T(8,128)S(1)}, f32[192,768]{1,0:T(8,128)}, u32[]{:S(2)}) copy-start(f32[192,768]{1,0:T(8,128)} %param.16) | copy-start | bytes 1769476
Sparse Core Ops, SparseCore 0:
  10.8 83.6 all-gather.3
  97.8 76.6 all-gather.5
  268.3 77.0 all-gather.7
where the time goes:
time: 432 us; the launch traced here: 431 us
  waiting for transfers between devices  222 us (51%)
  blocking collectives  158 us (37%)
  local copies, waits for them, and re-layouts  26 us (6%)
  between operations  14 us (3%)
  matrix products  7.02 us (2%)
    all_gather x1, waiting for transfers between devices, body(): all_u = lax.all_gather(flat_u, 'sub', axis=0, tiled=True)  77.2 us
    all_gather x1, waiting for transfers between devices, body(): lax.all_gather(flat_r, 'sub', axis=0, tiled=True)  77.1 us
    psum x1, blocking collectives, body(): coarse_residual = lax.psum(coarse_local, ('sub', 'crs'))  75.2 us
    psum x1, blocking collectives, body(): lax.psum(jnp.sum(residual * preconditioned), ('sub', 'crs')).reshape(1)  75.1 us
    all_gather x1, waiting for transfers between devices, body(): lax.all_gather(flat_k, 'sub', axis=0, tiled=True)  68 us
    reshape x1, local copies, waits for them, and re-layouts, body(): blocks = inverses.reshape(slots_here, faces, entries, patches_here, entries)  11.4 us
  transfers between devices with their start and end apart: 3, of which 3 were waited for; matrix products, arithmetic and copies ran while one was open for 5% of the time, Pallas kernels for 0%

commit v1 on v0

--- a/solution.py
+++ b/solution.py
@@ -74,7 +74,7 @@
         jnp.float32
     )
     coarse_local = jnp.einsum("sc,scn->n", coarse_part, onehot, precision=lax.Precision.HIGHEST)
-    coarse_residual = lax.psum(coarse_local, ("sub", "crs"))
+    coarse_residual = jnp.sum(lax.all_gather(coarse_local, ("sub", "crs")), axis=0)
     block_width = total_coarse // columns
     start = lax.axis_index("crs") * block_width
     block_part = lax.dynamic_slice_in_dim(coarse_residual, start, block_width)

time: 432 us -> 488 us (1.13)
  blocking collectives: 158 us -> 212 us
    all_gather x0 -> x1, blocking collectives: none -> 129 us  [body(): lax.all_gather(coarse_local, ('sub', 'crs'))]
    psum x1 -> x0, blocking collectives: 75.2 us -> none  [body(): coarse_residual = lax.psum(coarse_local, ('sub', 'crs'))]
  transfers between devices with their start and end apart: 3 -> 3, of which waited for: 3 -> 3; matrix products, arithmetic and copies ran while one was open for 5% -> 4% of each run, Pallas kernels for 0% -> 0%
where the time goes in v1:
time: 488 us
  waiting for transfers between devices  224 us (46%)
  blocking collectives  212 us (43%)
  local copies, waits for them, and re-layouts  26 us (5%)
  between operations  14 us (3%)
  matrix products  6.99 us (1%)
    all_gather x1, blocking collectives, body(): lax.all_gather(coarse_local, ('sub', 'crs'))  129 us
    all_gather x1, waiting for transfers between devices, body(): all_u = lax.all_gather(flat_u, 'sub', axis=0, tiled=True)  78.6 us
    all_gather x1, waiting for transfers between devices, body(): lax.all_gather(flat_r, 'sub', axis=0, tiled=True)  77.1 us
    psum x1, blocking collectives, body(): lax.psum(jnp.sum(residual * preconditioned), ('sub', 'crs')).reshape(1)  75.1 us
    all_gather x1, waiting for transfers between devices, body(): lax.all_gather(flat_k, 'sub', axis=0, tiled=True)  68 us
    reshape x1, local copies, waits for them, and re-layouts, body(): blocks = inverses.reshape(slots_here, faces, entries, patches_here, entries)  11.4 us
  transfers between devices with their start and end apart: 3, of which 3 were waited for; matrix products, arithmetic and copies ran while one was open for 4% of the time, Pallas kernels for 0%

profile of v1, /device:TPU:1, one launch (start us, length us, event | category | flops | bytes accessed | tf_op | source)
XLA Modules:
  0.0 487.6 jit_solution(8877000230276702285)
XLA Ops:
  7.2 0.0 all-gather.6.cloned.1.call-start
  7.2 1.0 copy.57
  8.2 0.6 reshape.60
  8.8 0.0 all-gather.6.cloned.1.call-update
  8.9 0.0 all-gather.8.cloned.1.call-start
  8.9 0.9 copy.60
  9.8 0.6 reshape.62
  10.5 0.0 all-gather.8.cloned.1.call-update
  10.5 0.0 all-gather.10.cloned.1.call-start
  10.5 0.7 fusion.12
  11.3 0.8 select_reduce_fusion.1
  12.1 0.5 select_reduce_fusion
  12.6 0.7 multiply_add_fusion
  13.3 0.1 copy.55
  13.5 0.1 add.182
  13.6 0.7 convert_element_type.12
  14.3 0.1 copy.58
  14.4 0.1 broadcast_in_dim.5
  14.5 0.1 reshape.61
  14.7 11.4 %copy.76 = bf16[4,6,192,768]{2,3,1,0:T(8,128)(2,1)} copy(bf16[4,6,192,768]{3,2,1,0:T(8,128)(2,1)} %param.12) | data formatting | bytes 14155776 | tf_op jit(solution)/shard_map/reshape | solution.py:61
  26.1 0.1 add.187
  26.2 0.1 add.188
  26.3 0.1 add.190
  26.4 0.1 compare_select_fusion
  26.4 68.0 %all-gather.6.cloned.1.call-done = f32[1536,768]{1,0:T(8,128)} async-done(((f32[24,768]{1,0:T(8,128)}), f32[1536,768]{1,0:T(8,128)}) %all-gather.6.cloned.1.call-update) | async-done | bytes 4718608 | tf_op jit(solution)/shard_map/all_gather | solution.py:54
  94.5 3.0 gather_fusion
  97.5 77.1 %all-gather.8.cloned.1.call-done = f32[1536,768]{1,0:T(8,128)} async-done(((f32[24,768]{1,0:T(8,128)}), f32[1536,768]{1,0:T(8,128)}) %all-gather.8.cloned.1.call-update) | async-done | bytes 4718608 | tf_op jit(solution)/shard_map/all_gather | solution.py:53
  174.5 3.0 gather_fusion.1
  177.5 0.1 fusion.3
  177.6 0.1 reshape.112
  177.7 5.1 %fusion.25 = f32[4,6,4,1,192]{4,3,2,1,0:T(1,128)S(1)} fusion(bf16[4,6,4,192,1]{3,4,2,1,0:T(2,128)(2,1)S(1)} %reshape.112, bf16[4,6,192,4,192]{2,4,3,1,0:T(8,128)(2,1)} %bitcast.43), kind=kOutput, calls=%fused_computation.85 | convolution fusion | flops 7077888 | bytes 7188480 | tf_op jit(solution)/shard_map/sfipj,sfpj->sfpi/dot_general | solution.py:63
  182.8 0.1 reshape.65
  183.0 0.4 convolution_bitcast_fusion.1
  183.4 0.3 convolution_bitcast_fusion
  183.7 129.4 %all-gather.1 = f32[256,1,768]{2,1,0:T(1,128)S(1)} all-gather(f32[1,1,768]{2,1,0:T(1,128)S(1)} %convolution_bitcast_fusion), channel_id=2, replica_groups=mesh['sub'=64,'crs'=4] {'sub','crs'}, dimensions={0}, use_global_device_ids=true | all-gather | bytes 789504 | tf_op jit(solution)/shard_map/all_gather | solution.py:77
  313.1 0.5 reduce_sum.38
  313.6 0.1 dynamic_slice.7
  313.7 0.4 convolution_reduce_fusion
  314.1 7.4 %psum.14 = f32[768]{0:T(1024)S(1)} all-reduce(f32[768]{0:T(1024)S(1)} %convolution_reduce_fusion), channel_id=1, replica_groups=mesh['sub'=64,'crs'=4] {'crs'}, use_global_device_ids=true, to_apply=%region_3.4 | all-reduce | flops 768 | bytes 6144 | tf_op jit(solution)/shard_map/psum | solution.py:82
  321.5 0.5 fusion
  322.0 0.3 fusion.7
  322.4 0.6 reshape.66
  323.0 0.0 all-gather.10.cloned.1.call-update
  323.1 78.6 %all-gather.10.cloned.1.call-done = f32[1536,768]{1,0:T(8,128)} async-done(((f32[24,768]{1,0:T(8,128)}), f32[1536,768]{1,0:T(8,128)}) %all-gather.10.cloned.1.call-update) | async-done | bytes 4718608 | tf_op jit(solution)/shard_map/all_gather | solution.py:91
  401.6 3.0 gather_fusion.2
  404.6 0.7 multiply_reduce_fusion
  405.3 0.7 copy.66
  405.9 75.1 %psum.15 = f32[1]{0:T(128)} all-reduce(f32[1]{0:T(128)} %bitcast.18), channel_id=1, replica_groups=mesh['sub'=64,'crs'=4] {'sub','crs'}, use_global_device_ids=true, to_apply=%region_5.6 | all-reduce | flops 1 | bytes 8 | tf_op jit(solution)/shard_map/psum | solution.py:94
  (23 shorter events, 0.2 us)
Async XLA Ops:
  7.2 175.8 %copy-start = (bf16[4,24,6,768]{3,1,2,0:T(8,128)(2,1)S(1)}, bf16[4,24,6,768]{3,1,2,0:T(8,128)(2,1)}, u32[]{:S(2)}) copy-start(bf16[4,24,6,768]{3,1,2,0:T(8,128)(2,1)} %param.13) | copy-start | bytes 2654212
  7.2 87.3 %all-gather.6.cloned.1.call-start = ((), (), s32[]{:S(2)}) async-start(), calls=%async_computation | async-start | bytes 4792320 | tf_op jit(solution)/shard_map/all_gather | solution.py:54
  8.9 165.7 %all-gather.8.cloned.1.call-start = ((), (), s32[]{:S(2)}) async-start(), calls=%async_computation.1 | async-start | bytes 4792320 | tf_op jit(solution)/shard_map/all_gather | solution.py:53
  10.5 391.1 %all-gather.10.cloned.1.call-start = ((), (), s32[]{:S(2)}) async-start(), calls=%async_computation.2 | async-start | bytes 4792320 | tf_op jit(solution)/shard_map/all_gather | solution.py:91
  14.7 11.4 %copy-start.4 = (s32[4,8]{1,0:T(4,128)S(1)}, s32[4,8]{1,0:T(4,128)}, u32[]{:S(2)}) copy-start(s32[4,8]{1,0:T(4,128)} %param.15) | copy-start | bytes 388
  14.7 162.9 %copy-start.1 = (f32[4,6,768]{2,0,1:T(4,128)S(1)}, f32[4,6,768]{2,0,1:T(4,128)}, u32[]{:S(2)}) copy-start(f32[4,6,768]{2,0,1:T(4,128)} %param.9) | copy-start | bytes 221188
  14.7 162.9 %copy-start.2 = (f32[4,6,768]{2,0,1:T(4,128)S(1)}, f32[4,6,768]{2,0,1:T(4,128)}, u32[]{:S(2)}) copy-start(f32[4,6,768]{2,0,1:T(4,128)} %param.10) | copy-start | bytes 221188
  177.7 135.9 %copy-start.3 = (f32[192,768]{1,0:T(8,128)S(1)}, f32[192,768]{1,0:T(8,128)}, u32[]{:S(2)}) copy-start(f32[192,768]{1,0:T(8,128)} %param.16) | copy-start | bytes 1769476
Sparse Core Ops, SparseCore 0:
  10.8 83.6 all-gather.5
  97.8 76.6 all-gather.7
  323.2 78.3 all-gather.9
